TPU v7x, 512 devices: a whole 4x8x8 slice. The times are simulated.
512 devices in a mesh: blk: 128 (over z, y, core), head: 4 (over x).
Axes of the slice: x: 4, y: 8, z: 8, core: 2. Of those that a mesh axis runs over, the one named last changes fastest.
Arguments:
- hidden_in: bfloat16 [512, 1024], P('blk'), may hold values from -6 to 6
- norm_gain: float32 [1024], replicated, may hold values from 0.25 to 1.75
- w_query: bfloat16 [1024, 1024], P(None, 'head'), may hold values from -0.1875 to 0.1875
- w_key: bfloat16 [1024, 1024], P(None, 'head'), may hold values from -0.1875 to 0.1875
- w_value: bfloat16 [1024, 1024], P(None, 'head'), may hold values from -0.1875 to 0.1875
- w_out: bfloat16 [1024, 1024], P('head'), may hold values from -0.1875 to 0.1875
- cache_keys: bfloat16 [256, 128, 1024], P('blk', None, 'head'), may hold values from -30 to 30
- cache_values: bfloat16 [256, 128, 1024], P('blk', None, 'head'), may hold values from -6 to 6
- block_node: int32 [256], P('blk'), may hold values from 0 to 167
- block_len: int32 [256], P('blk'), may hold values from 1 to 128, as said below
- live_count: int32 [128], P('blk'), may hold values from 1 to 2, as said below
- node_parent: int32 [168], replicated, may hold values from -1 to 39, as said below
- request_leaf: int32 [512], replicated, may hold values from 40 to 167
Outputs:
- hidden_out: bfloat16 [512, 1024], P('blk', 'head')
- new_keys: bfloat16 [512, 1024], P('blk', 'head')
- new_values: bfloat16 [512, 1024], P('blk', 'head')
Inputs may be any that keep to these rules, and one draw needn't show every extreme that they name: `block_len`: some block of every draw is full. `live_count`: some index of blk uses all its slots in every draw. `node_parent`: nodes 0 to 7 are roots (parent -1); a node of ids 8 to 39 has a root as parent; every later node has a second-level parent.
All inputs are finite; a program needn't handle non-finite values.
Results may differ from a plain program's by a relative error of at most 0.012.
The roundings to bfloat16 on the way count: a program that leaves them out, or rounds other values in their place, can miss the bound.
Values may be sent and summed in bfloat16 or wider, within the bound.
A program may use at most 64 MiB of HBM per device.

v0:
```python
import jax
import jax.numpy as jnp
from jax import lax
from jax.sharding import PartitionSpec as P

HD = 64


very_low = -1e30


def parent_of(node_ids, table):
    every_node = jnp.arange(table.shape[0], dtype=jnp.int32)
    picked = jnp.where(node_ids[:, None] == every_node[None, :], table[None, :], 0)
    return jnp.sum(picked, axis=1)


def shards(
    hidden_in,
    norm_gain,
    w_query,
    w_key,
    w_value,
    w_out,
    cache_keys,
    cache_values,
    block_node,
    block_len,
    live_count,
    node_parent,
    request_leaf,
):
    rows = hidden_in.shape[0]
    local_cols = w_query.shape[1]
    heads = local_cols // HD
    groups = lax.axis_size("blk")
    seq_len = cache_keys.shape[1]
    states = hidden_in.astype(jnp.float32)
    scale_inv = lax.rsqrt(jnp.mean(states * states, axis=1, keepdims=True) + 1e-06)
    normed = (states * scale_inv * norm_gain[None, :]).astype(jnp.bfloat16)
    query = jnp.dot(normed, w_query, preferred_element_type=jnp.float32).astype(jnp.bfloat16)
    key_new = jnp.dot(normed, w_key, preferred_element_type=jnp.float32).astype(jnp.bfloat16)
    value_new = jnp.dot(normed, w_value, preferred_element_type=jnp.float32).astype(jnp.bfloat16)
    everyone = lax.all_gather(query, "blk", axis=0, tiled=True)
    total_rows = everyone.shape[0]
    queries = everyone.reshape(total_rows, heads, HD)
    first = parent_of(request_leaf, node_parent)
    second = parent_of(first, node_parent)
    path = jnp.stack([request_leaf, first, second], axis=1)
    positions = jnp.arange(seq_len, dtype=jnp.int32)
    own_count = live_count[0]
    start = jnp.zeros((), jnp.int32)

    def fetch(turn):
        return (cache_keys[turn], cache_values[turn], block_node[turn], block_len[turn])

    def block_scores(turn):
        keys, values, node, length = fetch(turn)
        scores = jnp.einsum(
            "rhd,thd->rht",
            queries,
            keys.reshape(seq_len, heads, HD),
            preferred_element_type=jnp.float32,
        )
        seen = jnp.any(path == node, axis=1)
        valid = seen[:, None] & (positions < length)[None, :]
        return (
            jnp.where(valid[:, None, :], scores, very_low),
            valid,
            values.reshape(seq_len, heads, HD),
        )

    own_score = jnp.sum(
        query.reshape(rows, heads, HD).astype(jnp.float32)
        * key_new.reshape(rows, heads, HD).astype(jnp.float32),
        axis=2,
    )
    empty_max = jnp.full((total_rows, heads), very_low, jnp.float32)
    empty_denom = jnp.zeros((total_rows, heads), jnp.float32)
    empty_numer = jnp.zeros((total_rows, heads, HD), jnp.float32)

    def online(turn, carry):
        row_max, denom, numer = carry
        scores, valid, values = block_scores(turn)
        new_max = jnp.maximum(row_max, jnp.max(scores, axis=2))
        factor = jnp.exp(row_max - new_max)
        weights = jnp.where(valid[:, None, :], jnp.exp(scores - new_max[:, :, None]), 0.0)
        denom = denom * factor + jnp.sum(weights, axis=2)
        numer = numer * factor[:, :, None] + jnp.einsum(
            "rht,thd->rhd", weights.astype(jnp.bfloat16), values, preferred_element_type=jnp.float32
        )
        return (new_max, denom, numer)

    row_max, denom, numer = lax.fori_loop(
        start, own_count, online, (empty_max, empty_denom, empty_numer)
    )
    received = (
        lax.all_to_all(
            numer.reshape(groups, rows, local_cols), "blk", split_axis=0, concat_axis=0, tiled=True
        ),
        lax.all_to_all(
            row_max.reshape(groups, rows, heads), "blk", split_axis=0, concat_axis=0, tiled=True
        ),
        lax.all_to_all(
            denom.reshape(groups, rows, heads), "blk", split_axis=0, concat_axis=0, tiled=True
        ),
    )
    part_numer, part_max, part_denom = received
    top = jnp.maximum(jnp.max(part_max, axis=0), own_score)
    factor = jnp.exp(part_max - top[None])
    denom = jnp.sum(part_denom * factor, axis=0)
    numer = jnp.sum(part_numer.reshape(groups, rows, heads, HD) * factor[:, :, :, None], axis=0)
    own_weight = jnp.exp(own_score - top)
    denom = denom + own_weight
    numer = numer + own_weight.astype(jnp.bfloat16).astype(jnp.float32)[
        :, :, None
    ] * value_new.reshape(rows, heads, HD).astype(jnp.float32)
    attended = (numer / denom[:, :, None]).reshape(rows, local_cols).astype(jnp.bfloat16)
    partial_value = jnp.dot(attended, w_out, preferred_element_type=jnp.float32)
    summed = lax.psum_scatter(partial_value, "head", scatter_dimension=1, tiled=True)
    part_width = summed.shape[1]
    residual = lax.dynamic_slice_in_dim(states, lax.axis_index("head") * part_width, part_width, 1)
    return ((residual + summed).astype(jnp.bfloat16), key_new, value_new)


def solution(mesh):
    in_specs = (
        P("blk", None),
        P(),
        P(None, "head"),
        P(None, "head"),
        P(None, "head"),
        P("head", None),
        P("blk", None, "head"),
        P("blk", None, "head"),
        P("blk"),
        P("blk"),
        P("blk"),
        P(),
        P(),
    )
    out_specs = (P("blk", "head"), P("blk", "head"), P("blk", "head"))
    return jax.shard_map(shards, mesh=mesh, in_specs=in_specs, out_specs=out_specs, check_vma=False)
```

profile of v0, /device:TPU:8, one launch (start us, length us, event | category | flops | bytes accessed | tf_op | source)
XLA Modules:
  0.0 176.6 jit_solution(17560175385430543897)
XLA Ops:
  7.2 0.9 multiply_reduce_fusion.2
  8.1 1.3 convolution_convert_fusion.2
  9.4 56.3 %all-gather = bf16[128,4,256]{2,1,0:T(4,128)(2,1)S(1)} all-gather(bf16[1,4,256]{2,1,0:T(4,128)(2,1)S(1)} %bitcast.55), channel_id=1, replica_groups=mesh['blk'=128,'head'=4] {'blk'}, dimensions={0}, use_global_device_ids=true | all-gather | bytes 264192 | tf_op jit(solution)/shard_map/all_gather | solution.py:44
  65.6 0.3 reshape.94
  65.9 0.3 copy.63
  66.2 0.4 copy-done.4
  67.0 0.8 copy-done.1
  67.9 5.2 %while.15 = (s32[]{:T(128)}, f32[512,4]{0,1:T(4,128)S(1)}, f32[512,4]{0,1:T(4,128)S(1)}, f32[512,4,64]{0,2,1:T(8,128)S(1)}, s32[]{:T(128)}, /*index=5*/s32[2]{0:...) while((s32[]{:T(128)}, f32[512,4]{0,1:T(4,128)S(1)}, ...), condition=%wide.region_7.8_spmd.clone, body=%wide.region_3.7_spmd.clone.sunk | while | flops 69540480 | bytes 5512651 | solution.py:94
  68.5 0.6 dynamic_slice.27
  69.1 0.7 compare_reduce_fusion.2
  69.8 0.6 dynamic_slice.28
  70.4 0.6 iota_compare_fusion.4
  71.3 0.4 fusion.33
  72.0 0.4 fusion.35
  73.1 0.3 reshape.96
  73.3 0.9 copy.66
  74.2 10.6 %all-to-all-start.1 = ((f32[128,4,4]{1,2,0:T(4,128)}), f32[128,4,4]{1,2,0:T(4,128)S(1)}, u32[]{:S(2)}, u32[]{:S(2)}) async-start(f32[128,4,4]{1,2,0:T(4,128)} %copy.66), calls=%async_computation.1 | async-start | bytes 524288 | tf_op jit(solution)/shard_map/all_to_all | solution.py:101
  84.8 0.3 reshape.97
  85.1 0.9 copy.72
  86.0 13.6 %all-to-all-done.1 = f32[128,4,4]{1,2,0:T(4,128)S(1)} async-done(((f32[128,4,4]{1,2,0:T(4,128)}), f32[128,4,4]{1,2,0:T(4,128)S(1)}, u32[]{:S(2)}, u32[]{:S(2)}) %all-to-all-start.1) | async-done | bytes 8224 | tf_op jit(solution)/shard_map/all_to_all | solution.py:101
  99.5 6.1 %all-to-all-start.2 = ((f32[128,4,4]{1,2,0:T(4,128)}), f32[128,4,4]{1,2,0:T(4,128)S(1)}, u32[]{:S(2)}, u32[]{:S(2)}) async-start(f32[128,4,4]{1,2,0:T(4,128)} %copy.72), calls=%async_computation.2 | async-start | bytes 524288 | tf_op jit(solution)/shard_map/all_to_all | solution.py:104
  105.7 0.4 copy.65
  106.1 1.5 reshape.95
  107.5 12.9 %all-to-all-done.2 = f32[128,4,4]{1,2,0:T(4,128)S(1)} async-done(((f32[128,4,4]{1,2,0:T(4,128)}), f32[128,4,4]{1,2,0:T(4,128)S(1)}, u32[]{:S(2)}, u32[]{:S(2)}) %all-to-all-start.2) | async-done | bytes 8224 | tf_op jit(solution)/shard_map/all_to_all | solution.py:104
  120.5 6.1 %all-to-all-start = ((f32[128,4,256]{2,1,0:T(4,128)}), f32[128,4,256]{2,1,0:T(4,128)S(1)}, u32[]{:S(2)}, u32[]{:S(2)}) async-start(f32[128,4,256]{2,1,0:T(4,128)} %reshape.95), calls=%async_computation | async-start | bytes 1048576 | tf_op jit(solution)/shard_map/all_to_all | solution.py:98
  126.7 0.8 convert_multiply_fusion
  129.2 17.7 %all-to-all-done = f32[128,4,256]{2,1,0:T(4,128)S(1)} async-done(((f32[128,4,256]{2,1,0:T(4,128)}), f32[128,4,256]{2,1,0:T(4,128)S(1)}, u32[]{:S(2)}, u32[]{:S(2)}) %all-to-all-start) | async-done | bytes 524320 | tf_op jit(solution)/shard_map/all_to_all | solution.py:98
  146.9 0.3 multiply_reduce_fusion
  147.2 1.1 convolution_bitcast_fusion.2
  148.4 19.9 %reduce-scatter.4.cloned.1.call-done = f32[256,4]{1,0:T(8,128)} async-done(((f32[1024,4]{1,0:T(8,128)}), f32[256,4]{1,0:T(8,128)}) %reduce-scatter.4.cloned.1.call-update) | async-done | bytes 4112
  168.2 1.0 copy.76
  169.2 0.6 add_convert_fusion
  (57 shorter events, 2.8 us)
Async XLA Ops:
  7.2 140.0 %copy-start = (bf16[256,1024]{1,0:T(8,128)(2,1)S(1)}, bf16[256,1024]{1,0:T(8,128)(2,1)}, u32[]{:S(2)}) copy-start(bf16[256,1024]{1,0:T(8,128)(2,1)} %param.20) | copy-start | bytes 1572868
  7.2 0.9 copy-start.3
  65.9 0.7 copy-start.4
  65.9 0.7 copy-start.5
  66.9 0.9 copy-start.1
  66.9 1.0 copy-start.2
  67.0 0.9 copy-start.10
  67.0 0.9 copy-start.11
  74.2 25.3 %all-to-all-start.1 = ((f32[128,4,4]{1,2,0:T(4,128)}), f32[128,4,4]{1,2,0:T(4,128)S(1)}, u32[]{:S(2)}, u32[]{:S(2)}) async-start(f32[128,4,4]{1,2,0:T(4,128)} %copy.66), calls=%async_computation.1 | async-start | bytes 524288 | tf_op jit(solution)/shard_map/all_to_all | solution.py:101
  99.5 20.9 %all-to-all-start.2 = ((f32[128,4,4]{1,2,0:T(4,128)}), f32[128,4,4]{1,2,0:T(4,128)S(1)}, u32[]{:S(2)}, u32[]{:S(2)}) async-start(f32[128,4,4]{1,2,0:T(4,128)} %copy.72), calls=%async_computation.2 | async-start | bytes 524288 | tf_op jit(solution)/shard_map/all_to_all | solution.py:104
  107.5 19.1 %copy-start.7 = (bf16[1024,256]{1,0:T(8,128)(2,1)S(1)}, bf16[1024,256]{1,0:T(8,128)(2,1)}, u32[]{:S(2)}) copy-start(bf16[1024,256]{1,0:T(8,128)(2,1)} %param.18) | copy-start | bytes 1572868
  107.5 19.1 %copy-start.9 = (f32[1024]{0:T(1024)S(1)}, f32[1024]{0:T(1024)}, u32[]{:S(2)}) copy-start(f32[1024]{0:T(1024)} %param.16) | copy-start | bytes 12292
  120.5 26.4 %all-to-all-start = ((f32[128,4,256]{2,1,0:T(4,128)}), f32[128,4,256]{2,1,0:T(4,128)S(1)}, u32[]{:S(2)}, u32[]{:S(2)}) async-start(f32[128,4,256]{2,1,0:T(4,128)} %reshape.95), calls=%async_computation | async-start | bytes 1048576 | tf_op jit(solution)/shard_map/all_to_all | solution.py:98
  126.6 1.2 copy-start.8
  126.6 41.6 %reduce-scatter.4.cloned.1.call-start = ((), (), s32[]{:S(2)}) async-start(), calls=%async_computation.4 | async-start | bytes 655360
  127.9 19.2 %copy-start.6 = (bf16[4,256]{1,0:T(4,128)(2,1)}, bf16[4,256]{1,0:T(4,128)(2,1)S(1)}, u32[]{:S(2)}) copy-start(bf16[4,256]{1,0:T(4,128)(2,1)S(1)} %convolution_convert_fusion) | copy-start | bytes 6148
Sparse Core Ops, SparseCore 0:
  148.5 19.7 reduce-scatter.3
where the time goes:
time: 177 us
  waiting for transfers between devices  64 us (36%)
  blocking collectives  56.3 us (32%)
  starting transfers between devices  22.9 us (13%)
  between operations  14.3 us (8%)
  local copies, waits for them, and re-layouts  9.5 us (5%)
  matrix products  4.17 us (2%)
  other arithmetic  4.1 us (2%)
    all_gather x1, blocking collectives, shards(): everyone = lax.all_gather(query, 'blk', axis=0, tiled=True)  56.3 us
    unnamed x2, waiting for transfers between devices  19.9 us
    all_to_all x1, waiting for transfers between devices, shards(): lax.all_to_all(numer.reshape(groups, rows, local_cols), 'blk', split_axis...  17.7 us
    all_to_all x1, waiting for transfers between devices, shards(): lax.all_to_all(row_max.reshape(groups, rows, heads), 'blk', split_axis=0,...  13.6 us
    all_to_all x1, waiting for transfers between devices, shards(): lax.all_to_all(denom.reshape(groups, rows, heads), 'blk', split_axis=0, c...  12.9 us
    all_to_all x1, starting transfers between devices, shards(): lax.all_to_all(row_max.reshape(groups, rows, heads), 'blk', split_axis=0,...  10.6 us
    all_to_all x1, starting transfers between devices, shards(): lax.all_to_all(denom.reshape(groups, rows, heads), 'blk', split_axis=0, c...  6.1 us
    all_to_all x1, starting transfers between devices, shards(): lax.all_to_all(numer.reshape(groups, rows, local_cols), 'blk', split_axis...  6.1 us
  transfers between devices with their start and end apart: 4, of which 4 were waited for; matrix products, arithmetic and copies ran while one was open for 3% of the time, Pallas kernels for 0%

commit v1 on v0

v1 whole, which is shorter than its diff:
```python
import functools
import math

import jax
import jax.numpy as jnp
from jax import lax
from jax.experimental import pallas as pl
from jax.experimental.pallas import tpu as pltpu
from jax.sharding import PartitionSpec as P

HD = 64
RD = 4
BT = 128
SL = 2
W = 128
MESH = pl.DeviceIdType.MESH
F32 = jnp.float32
BF16 = jnp.bfloat16

very_low = -1e30
low_top = -1e29


def iota(shape, axis):
    return lax.broadcasted_iota(jnp.int32, shape, axis)


def dot_nt(a, b):
    return lax.dot_general(a, b, (((1,), (1,)), ((), ())), preferred_element_type=F32)


def dot(a, b):
    return jnp.dot(a, b, preferred_element_type=F32)


def kernel(
    side,
    heads_n,
    hidden_h,
    gain_h,
    parent_h,
    leaf_h,
    node_h,
    len_h,
    live_h,
    wq_h,
    wk_h,
    wv_h,
    wo_h,
    ck_h,
    cv_h,
    out,
    out_k,
    out_v,
    hidden,
    gain,
    parent,
    leaf,
    node,
    length,
    live,
    wq,
    wk,
    wv,
    wo,
    kbuf,
    vbuf,
    vt,
    hid8,
    g1,
    g2,
    meta_send,
    meta_recv,
    par,
    lim,
    r2s,
    r2,
    r3s,
    r3,
    xs,
    xr,
    res,
    lsem,
    csem,
    crem,
    g1s_sem,
    g1r_sem,
    g2s_sem,
    g2r_sem,
    r2s_sem,
    r2r_sem,
    r3s_sem,
    r3r_sem,
    xs_sem,
    xr_sem,
):
    n = side
    rows = n * 2 * RD
    lanes = 2 * rows
    nodes = par.shape[1]
    total = leaf.shape[1]
    me = lax.axis_index("blk")
    hd = lax.axis_index("head")
    core = me % 2
    y = (me // 2) % n
    z = me // (2 * n)
    flip = 1 - core
    a = y * flip + z * core
    b = z * flip + y * core

    def device(aa, bb, cc, hh):
        zz = bb * flip + aa * core
        yy = aa * flip + bb * core
        return {"blk": (zz * n + yy) * 2 + cc, "head": hh}

    def along_a(k):
        return device((a + k + n) % n, b, core, hd)

    def along_b(k):
        return device(a, (b + k + n) % n, core, hd)

    def along_x(k):
        return {"blk": me, "head": (hd + k) % heads_n}

    other = {"blk": me + 1 - 2 * core, "head": hd}

    barrier = pltpu.get_barrier_semaphore()
    for k in range(1, n):
        pl.semaphore_signal(barrier, inc=1, device_id=along_b(k), device_id_type=MESH)
    for k in range(1, n):
        pl.semaphore_signal(barrier, inc=1, device_id=along_a(k), device_id_type=MESH)
    pl.semaphore_signal(barrier, inc=1, device_id=other, device_id_type=MESH)
    for k in range(1, heads_n):
        pl.semaphore_signal(barrier, inc=1, device_id=along_x(k), device_id_type=MESH)

    loads = [
        pltpu.make_async_copy(src, dst, lsem.at[k])
        for k, (src, dst) in enumerate(
            [
                (hidden_h, hidden),
                (gain_h, gain),
                (wq_h, wq),
                (node_h, node),
                (len_h, length),
                (live_h, live),
                (wk_h, wk),
                (wv_h, wv),
                (cv_h, vbuf.at[pl.ds(0, SL)]),
                (ck_h, kbuf.at[pl.ds(0, SL)]),
                (parent_h, parent),
                (leaf_h, leaf),
                (wo_h, wo),
            ]
        )
    ]
    for load in loads:
        load.start()

    loads[0].wait()
    loads[1].wait()
    states = hidden[...].astype(F32)
    hid8[pl.ds(0, RD), :] = states
    hid8[pl.ds(RD, RD), :] = states
    h8 = hid8[...]
    inv = lax.rsqrt(jnp.mean(h8 * h8, axis=1, keepdims=True) + 1e-06)
    normed = (h8 * inv * gain[...]).astype(BF16)
    row8 = iota((2 * RD, W), 0)
    lane8 = iota((2 * RD, W), 1)
    upper = row8 < RD

    def tile_of(wide):
        return jnp.where(upper, wide[:, 0:W], wide[:, W : 2 * W])

    loads[2].wait()
    q8 = tile_of(dot(normed, wq[...]).astype(BF16).astype(F32))
    g1[0] = q8

    for k in (3, 4, 5):
        loads[k].wait()
    own_len = [jnp.where(s < live[:, 0:1], length[:, s : s + 1], 0).astype(F32) for s in range(SL)]
    own_node = [node[:, s : s + 1].astype(F32) for s in range(SL)]

    def slot_tile(first):
        tile = jnp.zeros((8, W), F32)
        for s in range(SL):
            tile = jnp.where(row8 == first + s, own_node[s], tile)
            tile = jnp.where(row8 == 4 + first + s, own_len[s], tile)
        return tile

    meta_send[...] = slot_tile(SL)

    sends = []

    def send(src, dst, send_sem, recv_sem, target):
        copy = pltpu.make_async_remote_copy(
            src_ref=src,
            dst_ref=dst,
            send_sem=send_sem,
            recv_sem=recv_sem,
            device_id=target,
            device_id_type=MESH,
        )
        copy.start()
        sends.append(copy)
        return copy

    pl.semaphore_wait(barrier, 2 * (n - 1) + 1 + heads_n - 1)

    order = sorted(range(1, n), key=lambda k: -min(k, n - k))
    got1 = {k: send(g1.at[0], g1.at[k], g1s_sem.at[k], g1r_sem.at[k], along_b(k)) for k in order}
    got_meta = send(meta_send, meta_recv, csem.at[0], crem.at[0], other)
    got_v = send(cv_h, vbuf.at[pl.ds(SL, SL)], csem.at[1], crem.at[1], other)
    got_k = send(ck_h, kbuf.at[pl.ds(SL, SL)], csem.at[2], crem.at[2], other)

    loads[6].wait()
    k8 = dot(normed, wk[...]).astype(BF16)
    out_k[...] = k8[0:RD, :]
    loads[7].wait()
    v8 = dot(normed, wv[...]).astype(BF16)
    out_v[...] = v8[0:RD, :]
    k8 = tile_of(k8.astype(F32))
    v8 = tile_of(v8.astype(F32))
    prod = q8 * k8
    left = lane8 < HD
    own = jnp.where(
        left,
        jnp.sum(jnp.where(left, prod, 0.0), axis=1, keepdims=True),
        jnp.sum(jnp.where(left, 0.0, prod), axis=1, keepdims=True),
    )
    for k in range(heads_n):
        res[k] = tile_of(h8[:, 2 * W * k : 2 * W * (k + 1)])

    for k in range(1, n):
        got1[k].wait_recv()
    g2[0] = g1[...].reshape(rows, W).astype(BF16)
    got2 = {k: send(g2.at[0], g2.at[k], g2s_sem.at[k], g2r_sem.at[k], along_a(k)) for k in order}

    loads[10].wait()
    loads[11].wait()
    par[...] = jnp.full_like(par, -1.0)
    par[:, 0 : parent.shape[1]] = parent[...].astype(F32)
    node_of_row = iota((nodes, 1), 0).astype(F32)
    hop = jnp.where(node_of_row == par[...], 1.0, 0.0).astype(BF16)
    leaf_hot = jnp.where(node_of_row == leaf[...].astype(F32), 1.0, 0.0).astype(BF16)
    spot = iota((1, n * lanes), 1)
    at_i = lax.rem(a + n - spot // lanes, n)
    at_j = lax.rem(b + n - lax.rem(spot // (2 * RD), n), n)
    at_z = at_j * flip + at_i * core
    at_y = at_i * flip + at_j * core
    request = ((at_z * n + at_y) * 2 + core) * RD + lax.rem(spot, RD)
    pick = jnp.where(iota((total, 1), 0) == request, 1.0, 0.0).astype(BF16)

    got_meta.wait_recv()
    slots = slot_tile(0) + meta_recv[...]
    slot_node = jnp.concatenate([slots] * (nodes // W), axis=1)
    slot_len = jnp.concatenate([pltpu.roll(slots, 4, 0)] * (nodes // W), axis=1)
    level = jnp.where(iota((8, nodes), 1).astype(F32) == slot_node, 1.0, 0.0)
    up1 = dot(level.astype(BF16), hop)
    up2 = dot(up1.astype(BF16), hop)
    limits = ((level + up1 + up2) * slot_len).astype(BF16)
    limits = dot(limits, leaf_hot).astype(BF16)
    lim[...] = dot(limits, pick)

    loads[8].wait()
    got_v.wait_recv()
    vt[...] = vbuf[...].reshape(2 * SL * BT, 2 * W).astype(F32).T.astype(BF16)
    loads[9].wait()
    got_k.wait_recv()
    keys = kbuf[...].reshape(2 * SL * BT, 2 * W)

    spread_row = iota((lanes, 2 * W), 0)
    spread_lane = iota((lanes, 2 * W), 1)
    spread = jnp.where(
        (spread_row // rows == lax.rem(spread_lane // HD, 2)) & (lax.rem(spread_row // RD, 2) == spread_lane // W),
        1.0,
        0.0,
    ).astype(BF16)
    lane1 = iota((1, lanes), 1)
    lane_head = 2 * lax.rem(lane1 // RD, 2) + lane1 // rows
    token = iota((BT, lanes), 0).astype(F32)
    row16 = iota((16, lanes), 0)

    def partial(k):
        block = g2[k]
        block = jnp.concatenate([block, block], axis=1)
        queries = jnp.concatenate([block, block], axis=0) * spread
        scores = dot_nt(keys, queries)
        parts = []
        for s in range(2 * SL):
            limit = lim[s : s + 1, k * lanes : (k + 1) * lanes]
            parts.append(jnp.where(token < limit, scores[s * BT : (s + 1) * BT], very_low))
        masked = jnp.concatenate(parts, axis=0)
        top = jnp.maximum(jnp.max(masked, axis=0, keepdims=True), low_top)
        top_hi = top.astype(BF16).astype(F32)
        top_lo = (top - top_hi).astype(BF16).astype(F32)
        weights = jnp.exp(masked - (top_hi + top_lo))
        denom = jnp.sum(weights, axis=0, keepdims=True)
        full = dot(vt[...], weights.astype(BF16))
        numer = full[0:HD]
        for h in range(1, 4):
            numer = jnp.where(lane_head == h, full[h * HD : (h + 1) * HD], numer)
        den_hi = denom.astype(BF16).astype(F32)
        den_lo = denom - den_hi
        stats = jnp.where(
            row16 == 0,
            top_hi,
            jnp.where(row16 == 1, top_lo, jnp.where(row16 == 2, den_hi, den_lo)),
        )
        return numer.astype(BF16), stats.astype(BF16)

    got3 = {}
    for k in [0] + order[::-1]:
        if k:
            got2[k].wait_recv()
        numer, stats = partial(k)
        target = r2s.at[k] if k else r2.at[0]
        target[0:HD, :] = numer
        target[HD : HD + 16, :] = stats
        if k:
            got3[k] = send(r2s.at[k], r2.at[k], r2s_sem.at[k], r2r_sem.at[k], along_a(-k))

    for k in order:
        got3[k].wait_recv()
    stats = [r2[k, HD : HD + 16, :].astype(F32) for k in range(n)]
    tops = [s[0:1] + s[1:2] for s in stats]
    top = functools.reduce(jnp.maximum, tops)
    numer = jnp.zeros((HD, lanes), F32)
    denom = jnp.zeros((1, lanes), F32)
    for k in range(n):
        factor = jnp.exp(tops[k] - top)
        denom = denom + (stats[k][2:3] + stats[k][3:4]) * factor
        numer = numer + r2[k, 0:HD, :].astype(F32) * factor

    first = iota((HD, lanes), 1) < rows

    def turn(x):
        x = jnp.concatenate([jnp.where(first, x, 0.0), jnp.where(first, 0.0, x)], axis=0).T
        return x[0:rows] + x[rows : 2 * rows]

    numer = turn(numer)
    both = turn(jnp.where(iota((HD, lanes), 0) < HD // 2, top, denom))
    for k in range(n):
        target = r3s.at[k] if k else r3.at[0]
        target[0:8, :] = numer[8 * k : 8 * k + 8]
        target[8:16, :] = both[8 * k : 8 * k + 8]
    got4 = {k: send(r3s.at[k], r3.at[k], r3s_sem.at[k], r3r_sem.at[k], along_b(-k)) for k in order}
    loads[12].wait()
    for k in order:
        got4[k].wait_recv()
    near = lax.rem(lane8, HD) < HD // 2
    tops, denoms = [], []
    for k in range(n):
        both = r3[k, 8:16, :]
        tops.append(jnp.where(near, both, pltpu.roll(both, HD // 2, 1)))
        denoms.append(jnp.where(near, pltpu.roll(both, W - HD // 2, 1), both))
    top = functools.reduce(jnp.maximum, tops, own)
    own_weight = jnp.exp(own - top)
    denom = own_weight
    numer = own_weight.astype(BF16).astype(F32) * v8
    for k in range(n):
        factor = jnp.exp(tops[k] - top)
        denom = denom + denoms[k] * factor
        numer = numer + r3[k, 0:8, :] * factor
    attended = (numer / denom).astype(BF16).astype(F32)
    attended = jnp.concatenate([jnp.where(upper, attended, 0.0), jnp.where(upper, 0.0, attended)], axis=1)
    part = dot(attended.astype(BF16), wo[...])
    part = part + pltpu.roll(part, RD, 0)
    for k in range(heads_n):
        xs[k] = tile_of(part[:, 2 * W * k : 2 * W * (k + 1)])
    got5 = [
        send(xs.at[(hd + k) % heads_n], xr.at[k], xs_sem.at[k], xr_sem.at[k], along_x(k)) for k in range(1, heads_n)
    ]
    summed = xs[hd]
    for k in range(1, heads_n):
        got5[k - 1].wait_recv()
        summed = summed + xr[k]
    summed = (summed + res[hd]).astype(BF16)
    out[:, 0:W] = summed[0:RD]
    out[:, W : 2 * W] = summed[RD : 2 * RD]
    for copy in sends:
        copy.wait_send()


def shards(
    hidden_in,
    norm_gain,
    w_query,
    w_key,
    w_value,
    w_out,
    cache_keys,
    cache_values,
    block_node,
    block_len,
    live_count,
    node_parent,
    request_leaf,
):
    side = math.isqrt(lax.axis_size("blk") // 2)
    heads_n = lax.axis_size("head")
    d_model = hidden_in.shape[1]
    cols = w_query.shape[1]
    n = side
    rows = n * 2 * RD
    lanes = 2 * rows
    nodes = -(-node_parent.shape[0] // W) * W
    vmem = pl.BlockSpec(memory_space=pltpu.VMEM)
    hbm = pl.BlockSpec(memory_space=pltpu.HBM)
    shape = jax.ShapeDtypeStruct
    new = shape((RD, cols), BF16)
    dma = pltpu.SemaphoreType.DMA
    return pl.pallas_call(
        functools.partial(kernel, side, heads_n),
        out_shape=(new, new, new),
        in_specs=[hbm] * 13,
        out_specs=(vmem, vmem, vmem),
        scratch_shapes=[
            pltpu.VMEM((RD, d_model), BF16),
            pltpu.VMEM((1, d_model), F32),
            pltpu.VMEM((1, node_parent.shape[0]), jnp.int32),
            pltpu.VMEM((1, request_leaf.shape[0]), jnp.int32),
            pltpu.VMEM((1, SL), jnp.int32),
            pltpu.VMEM((1, SL), jnp.int32),
            pltpu.VMEM((1, 1), jnp.int32),
            pltpu.VMEM((d_model, cols), BF16),
            pltpu.VMEM((d_model, cols), BF16),
            pltpu.VMEM((d_model, cols), BF16),
            pltpu.VMEM((cols, d_model), BF16),
            pltpu.VMEM((2 * SL, BT, cols), BF16),
            pltpu.VMEM((2 * SL, BT, cols), BF16),
            pltpu.VMEM((cols, 2 * SL * BT), BF16),
            pltpu.VMEM((2 * RD, d_model), F32),
            pltpu.VMEM((n, 2 * RD, W), F32),
            pltpu.VMEM((n, rows, W), BF16),
            pltpu.VMEM((8, W), F32),
            pltpu.VMEM((8, W), F32),
            pltpu.VMEM((1, nodes), F32),
            pltpu.VMEM((8, n * lanes), F32),
            pltpu.VMEM((n, HD + 16, lanes), BF16),
            pltpu.VMEM((n, HD + 16, lanes), BF16),
            pltpu.VMEM((n, 16, W), F32),
            pltpu.VMEM((n, 16, W), F32),
            pltpu.VMEM((heads_n, 8, W), F32),
            pltpu.VMEM((heads_n, 8, W), F32),
            pltpu.VMEM((heads_n, 8, W), F32),
            dma((13,)),
            dma((3,)),
            dma((3,)),
        ]
        + [dma((n,))] * 8
        + [dma((heads_n,))] * 2,
        compiler_params=pltpu.CompilerParams(
            collective_id=0, has_side_effects=True, vmem_limit_bytes=60 * 1024 * 1024
        ),
    )(
        hidden_in,
        norm_gain.reshape(1, -1),
        node_parent.reshape(1, -1),
        request_leaf.reshape(1, -1),
        block_node.reshape(1, -1),
        block_len.reshape(1, -1),
        live_count.reshape(1, -1),
        w_query,
        w_key,
        w_value,
        w_out,
        cache_keys,
        cache_values,
    )


def solution(mesh):
    in_specs = (
        P("blk", None),
        P(),
        P(None, "head"),
        P(None, "head"),
        P(None, "head"),
        P("head", None),
        P("blk", None, "head"),
        P("blk", None, "head"),
        P("blk"),
        P("blk"),
        P("blk"),
        P(),
        P(),
    )
    out_specs = (P("blk", "head"), P("blk", "head"), P("blk", "head"))
    return jax.shard_map(shards, mesh=mesh, in_specs=in_specs, out_specs=out_specs, check_vma=False)
```

time: 177 us -> 45.2 us (0.26)
  the two profiles are of different devices: /device:TPU:8 before, /device:TPU:24 now
where the time goes in v1:
time: 45.2 us; the launch traced here: 45 us
  Pallas kernels  41.1 us (91%)
  local copies, waits for them, and re-layouts  2.57 us (6%)
  between operations  1.3 us (3%)
    pallas_call x1, Pallas kernels, shards(): pl.pallas_call(functools.partial(kernel, side, heads_n), out_shape=(new,...  41.1 us
    unnamed x9, local copies, waits for them, and re-layouts  2.57 us

profile of v1, /device:TPU:24, one launch (start us, length us, event | category | flops | bytes accessed | tf_op | source)
XLA Modules:
  0.0 45.0 jit_solution(4178307861488088992)
XLA Ops:
  1.3 41.1 %shard_map.148 = (bf16[4,256]{1,0:T(4,128)(2,1)}, bf16[4,256]{1,0:T(4,128)(2,1)}, bf16[4,256]{1,0:T(4,128)(2,1)}) custom-call(bf16[4,1024]{1,0:T(4,128)(2,1)} %hidden_h.1, f32[1,1024]{1,0:T(1,128)} %bitcast.7, s32[1,168]{1,0:T(1,128)} %bitcast.9, s32[1,512]{1,0:T(1,128)} %bitcast.8, s32[1,2]{1,0:T(1,128)} %bitcast.10, s32[1,2]{1,0:T(1,128)} %bitcast.11, ...), custom_call_target="tpu_custom_call" | custom-call | tf_op jit(solution)/shard_map/pallas_call | solution.py:412
  42.4 0.0 copy-start.2
  42.4 0.6 %copy-done.2 = bf16[4,256]{1,0:T(4,128)(2,1)S(1)} copy-done((bf16[4,256]{1,0:T(4,128)(2,1)S(1)}, bf16[4,256]{1,0:T(4,128)(2,1)}, u32[]{:S(2)}) %copy-start.2) | copy-done | bytes 2072
  43.0 0.0 copy-start.1
  43.0 0.6 %copy.20 = bf16[4,256]{1,0:T(4,128)(2,1)} copy(bf16[4,256]{1,0:T(4,128)(2,1)S(1)} %copy-done.2) | data formatting | bytes 4096
  43.6 0.1 copy-done.1
  43.7 0.0 copy-start
  43.7 0.6 %copy.21 = bf16[4,256]{1,0:T(4,128)(2,1)} copy(bf16[4,256]{1,0:T(4,128)(2,1)S(1)} %copy-done.1) | data formatting | bytes 4096
  44.3 0.1 copy-done
  44.4 0.6 %copy.22 = bf16[4,256]{1,0:T(4,128)(2,1)} copy(bf16[4,256]{1,0:T(4,128)(2,1)S(1)} %copy-done) | data formatting | bytes 4096
Async XLA Ops:
  42.4 0.7 %copy-start.2 = (bf16[4,256]{1,0:T(4,128)(2,1)S(1)}, bf16[4,256]{1,0:T(4,128)(2,1)}, u32[]{:S(2)}) copy-start(bf16[4,256]{1,0:T(4,128)(2,1)} %get-tuple-element.6) | copy-start | bytes 6148
  43.0 0.7 %copy-start.1 = (bf16[4,256]{1,0:T(4,128)(2,1)S(1)}, bf16[4,256]{1,0:T(4,128)(2,1)}, u32[]{:S(2)}) copy-start(bf16[4,256]{1,0:T(4,128)(2,1)} %get-tuple-element.7) | copy-start | bytes 6148
  43.7 0.7 %copy-start = (bf16[4,256]{1,0:T(4,128)(2,1)S(1)}, bf16[4,256]{1,0:T(4,128)(2,1)}, u32[]{:S(2)}) copy-start(bf16[4,256]{1,0:T(4,128)(2,1)} %get-tuple-element.8) | copy-start | bytes 6148

commit v2 on v1

--- a/solution.py
+++ b/solution.py
@@ -19,6 +19,7 @@
 
 very_low = -1e30
 low_top = -1e29
+BATCHES8 = ((0, 1, 7), (2, 6), (3, 5, 4))
 
 
 def iota(shape, axis):
@@ -49,9 +50,7 @@
     wo_h,
     ck_h,
     cv_h,
-    out,
-    out_k,
-    out_v,
+    outs,
     hidden,
     gain,
     parent,
@@ -65,18 +64,16 @@
     wo,
     kbuf,
     vbuf,
-    vt,
     hid8,
     g1,
     g2,
     meta_send,
     meta_recv,
     par,
-    lim,
-    r2s,
-    r2,
-    r3s,
-    r3,
+    pick,
+    bias,
+    back_s,
+    back,
     xs,
     xr,
     res,
@@ -87,10 +84,8 @@
     g1r_sem,
     g2s_sem,
     g2r_sem,
-    r2s_sem,
-    r2r_sem,
-    r3s_sem,
-    r3r_sem,
+    bs_sem,
+    br_sem,
     xs_sem,
     xr_sem,
 ):
@@ -108,16 +103,19 @@
     a = y * flip + z * core
     b = z * flip + y * core
 
-    def device(aa, bb, cc, hh):
-        zz = bb * flip + aa * core
-        yy = aa * flip + bb * core
-        return {"blk": (zz * n + yy) * 2 + cc, "head": hh}
+    step_a = 2 * flip + 2 * n * core
+    step_b = 2 * n * flip + 2 * core
+    base_a = [(a + k) % n * step_a + core for k in range(n)]
+    base_b = [(b + k) % n * step_b for k in range(n)]
+
+    def plane(k, j):
+        return {"blk": base_a[k % n] + base_b[j % n], "head": hd}
 
     def along_a(k):
-        return device((a + k + n) % n, b, core, hd)
+        return plane(k, 0)
 
     def along_b(k):
-        return device(a, (b + k + n) % n, core, hd)
+        return plane(0, k)
 
     def along_x(k):
         return {"blk": me, "head": (hd + k) % heads_n}
@@ -191,7 +189,7 @@
 
     sends = []
 
-    def send(src, dst, send_sem, recv_sem, target):
+    def send(src, dst, send_sem, recv_sem, target, alone=True):
         copy = pltpu.make_async_remote_copy(
             src_ref=src,
             dst_ref=dst,
@@ -201,7 +199,8 @@
             device_id_type=MESH,
         )
         copy.start()
-        sends.append(copy)
+        if alone:
+            sends.append(copy)
         return copy
 
     pl.semaphore_wait(barrier, 2 * (n - 1) + 1 + heads_n - 1)
@@ -214,10 +213,10 @@
 
     loads[6].wait()
     k8 = dot(normed, wk[...]).astype(BF16)
-    out_k[...] = k8[0:RD, :]
+    outs[1] = k8[0:RD, :]
     loads[7].wait()
     v8 = dot(normed, wv[...]).astype(BF16)
-    out_v[...] = v8[0:RD, :]
+    outs[2] = v8[0:RD, :]
     k8 = tile_of(k8.astype(F32))
     v8 = tile_of(v8.astype(F32))
     prod = q8 * k8
@@ -230,6 +229,14 @@
     for k in range(heads_n):
         res[k] = tile_of(h8[:, 2 * W * k : 2 * W * (k + 1)])
 
+    spot = iota((n * rows, 1), 0)
+    at_i = lax.rem(a + n - spot // rows, n)
+    at_j = lax.rem(b + n - lax.rem(spot // (2 * RD), n), n)
+    at_z = at_j * flip + at_i * core
+    at_y = at_i * flip + at_j * core
+    request = ((at_z * n + at_y) * 2 + core) * RD + lax.rem(spot, RD)
+    pick[...] = jnp.where(iota((1, total), 1) == request, 1.0, 0.0).astype(BF16)
+
     for k in range(1, n):
         got1[k].wait_recv()
     g2[0] = g1[...].reshape(rows, W).astype(BF16)
@@ -242,14 +249,6 @@
     node_of_row = iota((nodes, 1), 0).astype(F32)
     hop = jnp.where(node_of_row == par[...], 1.0, 0.0).astype(BF16)
     leaf_hot = jnp.where(node_of_row == leaf[...].astype(F32), 1.0, 0.0).astype(BF16)
-    spot = iota((1, n * lanes), 1)
-    at_i = lax.rem(a + n - spot // lanes, n)
-    at_j = lax.rem(b + n - lax.rem(spot // (2 * RD), n), n)
-    at_z = at_j * flip + at_i * core
-    at_y = at_i * flip + at_j * core
-    request = ((at_z * n + at_y) * 2 + core) * RD + lax.rem(spot, RD)
-    pick = jnp.where(iota((total, 1), 0) == request, 1.0, 0.0).astype(BF16)
-
     got_meta.wait_recv()
     slots = slot_tile(0) + meta_recv[...]
     slot_node = jnp.concatenate([slots] * (nodes // W), axis=1)
@@ -257,16 +256,29 @@
     level = jnp.where(iota((8, nodes), 1).astype(F32) == slot_node, 1.0, 0.0)
     up1 = dot(level.astype(BF16), hop)
     up2 = dot(up1.astype(BF16), hop)
-    limits = ((level + up1 + up2) * slot_len).astype(BF16)
-    limits = dot(limits, leaf_hot).astype(BF16)
-    lim[...] = dot(limits, pick)
+    seen = dot((level + up1 + up2).astype(BF16), leaf_hot)
+    row_of = iota((8, total), 0)
+    unseen = jnp.where(row_of < 2 * SL, 1.0 - seen, jnp.where(row_of == 2 * SL, 1.0, 0.0))
+    unseen = jnp.concatenate([unseen, jnp.zeros((W - 8, total), F32)], axis=0).astype(BF16)
+    unseen = dot_nt(pick[...], unseen).astype(BF16)
+    spot1 = iota((1, BT), 1).astype(F32)
+    ends = [jnp.where(spot1 < slots[4 + s : 5 + s, :], 0.0, very_low) for s in range(2 * SL)]
+    ends = jnp.concatenate(ends, axis=1)
+    tokens = 2 * SL * BT
+    slot_row = iota((W, tokens), 0)
+    hide = jnp.where(
+        slot_row == 2 * SL,
+        ends,
+        jnp.where(slot_row == iota((W, tokens), 1) // BT, very_low, 0.0),
+    ).astype(BF16)
+    bias[...] = dot(unseen, hide).reshape(n, rows, tokens)
 
     loads[8].wait()
     got_v.wait_recv()
-    vt[...] = vbuf[...].reshape(2 * SL * BT, 2 * W).astype(F32).T.astype(BF16)
+    values = vbuf[...].reshape(tokens, 2 * W)
     loads[9].wait()
     got_k.wait_recv()
-    keys = kbuf[...].reshape(2 * SL * BT, 2 * W)
+    keys = kbuf[...].reshape(tokens, 2 * W)
 
     spread_row = iota((lanes, 2 * W), 0)
     spread_lane = iota((lanes, 2 * W), 1)
@@ -275,92 +287,81 @@
         1.0,
         0.0,
     ).astype(BF16)
-    lane1 = iota((1, lanes), 1)
-    lane_head = 2 * lax.rem(lane1 // RD, 2) + lane1 // rows
-    token = iota((BT, lanes), 0).astype(F32)
-    row16 = iota((16, lanes), 0)
-
-    def partial(k):
-        block = g2[k]
-        block = jnp.concatenate([block, block], axis=1)
-        queries = jnp.concatenate([block, block], axis=0) * spread
-        scores = dot_nt(keys, queries)
-        parts = []
-        for s in range(2 * SL):
-            limit = lim[s : s + 1, k * lanes : (k + 1) * lanes]
-            parts.append(jnp.where(token < limit, scores[s * BT : (s + 1) * BT], very_low))
-        masked = jnp.concatenate(parts, axis=0)
-        top = jnp.maximum(jnp.max(masked, axis=0, keepdims=True), low_top)
-        top_hi = top.astype(BF16).astype(F32)
-        top_lo = (top - top_hi).astype(BF16).astype(F32)
-        weights = jnp.exp(masked - (top_hi + top_lo))
-        denom = jnp.sum(weights, axis=0, keepdims=True)
-        full = dot(vt[...], weights.astype(BF16))
-        numer = full[0:HD]
-        for h in range(1, 4):
-            numer = jnp.where(lane_head == h, full[h * HD : (h + 1) * HD], numer)
-        den_hi = denom.astype(BF16).astype(F32)
-        den_lo = denom - den_hi
-        stats = jnp.where(
-            row16 == 0,
-            top_hi,
-            jnp.where(row16 == 1, top_lo, jnp.where(row16 == 2, den_hi, den_lo)),
-        )
-        return numer.astype(BF16), stats.astype(BF16)
-
-    got3 = {}
-    for k in [0] + order[::-1]:
-        if k:
-            got2[k].wait_recv()
-        numer, stats = partial(k)
-        target = r2s.at[k] if k else r2.at[0]
-        target[0:HD, :] = numer
-        target[HD : HD + 16, :] = stats
-        if k:
-            got3[k] = send(r2s.at[k], r2.at[k], r2s_sem.at[k], r2r_sem.at[k], along_a(-k))
-
-    for k in order:
-        got3[k].wait_recv()
-    stats = [r2[k, HD : HD + 16, :].astype(F32) for k in range(n)]
-    tops = [s[0:1] + s[1:2] for s in stats]
-    top = functools.reduce(jnp.maximum, tops)
-    numer = jnp.zeros((HD, lanes), F32)
-    denom = jnp.zeros((1, lanes), F32)
-    for k in range(n):
-        factor = jnp.exp(tops[k] - top)
-        denom = denom + (stats[k][2:3] + stats[k][3:4]) * factor
-        numer = numer + r2[k, 0:HD, :].astype(F32) * factor
-
-    first = iota((HD, lanes), 1) < rows
-
-    def turn(x):
-        x = jnp.concatenate([jnp.where(first, x, 0.0), jnp.where(first, 0.0, x)], axis=0).T
-        return x[0:rows] + x[rows : 2 * rows]
-
-    numer = turn(numer)
-    both = turn(jnp.where(iota((HD, lanes), 0) < HD // 2, top, denom))
-    for k in range(n):
-        target = r3s.at[k] if k else r3.at[0]
-        target[0:8, :] = numer[8 * k : 8 * k + 8]
-        target[8:16, :] = both[8 * k : 8 * k + 8]
-    got4 = {k: send(r3s.at[k], r3.at[k], r3s_sem.at[k], r3r_sem.at[k], along_b(-k)) for k in order}
+    low_half = lax.rem(iota((lanes, W), 0), 2 * RD) < RD
+    lane = iota((rows, W), 1)
+    first = lane < HD
+    part_of = lax.rem(lane, HD) // 16
+
+    def pair(x):
+        return jnp.where(first, x[0:rows], x[rows : 2 * rows])
+
+    def split(x):
+        hi = x.astype(BF16).astype(F32)
+        return hi, (x - hi).astype(BF16).astype(F32)
+
+    def attend(batch):
+        queries, hidden_bias = [], []
+        for k in batch:
+            block = g2[k]
+            block = jnp.concatenate([block, block], axis=1)
+            queries.append(jnp.concatenate([block, block], axis=0) * spread)
+            hidden_bias += [bias[k], bias[k]]
+        scores = dot_nt(jnp.concatenate(queries, axis=0), keys) + jnp.concatenate(hidden_bias, axis=0)
+        top_hi, top_lo = split(jnp.maximum(jnp.max(scores, axis=1, keepdims=True), low_top))
+        weights = jnp.exp(scores - (top_hi + top_lo))
+        den_hi, den_lo = split(jnp.sum(weights, axis=1, keepdims=True))
+        full = dot(weights.astype(BF16), values)
+        for at, k in enumerate(batch):
+            here = slice(at * lanes, (at + 1) * lanes)
+            numer = pair(jnp.where(low_half, full[here, 0:W], full[here, W : 2 * W]))
+            stats = jnp.where(
+                part_of == 0,
+                pair(top_hi[here]),
+                jnp.where(part_of == 1, pair(top_lo[here]), jnp.where(part_of == 2, pair(den_hi[here]), pair(den_lo[here]))),
+            )
+            both = jnp.concatenate([numer.reshape(n, 8, W), stats.reshape(n, 8, W)], axis=1).astype(BF16)
+            if k:
+                back_s[n * k : n * (k + 1)] = both
+            else:
+                back_s[1:n] = both[1:n]
+                back[0] = both[0]
+
+    returned = None
+    reach = [min(k, n - k) for k in range(n)]
+    batches = BATCHES8 if n == 8 else (tuple(range(n)),)
+    for batch in batches:
+        for k in batch:
+            if k:
+                got2[k].wait_recv()
+        attend(batch)
+        pairs = [(k, j) for k in batch for j in range(n) if k or j]
+        for k, j in sorted(pairs, key=lambda p: -reach[p[0]] - reach[p[1]]):
+            slot = n * k + j
+            send(back_s.at[slot], back.at[slot], bs_sem, br_sem, plane(-k, -j), False)
+    others = pl.ds(1, n * n - 1)
+    all_back = pltpu.make_async_copy(back_s.at[others], back.at[others], br_sem)
     loads[12].wait()
-    for k in order:
-        got4[k].wait_recv()
-    near = lax.rem(lane8, HD) < HD // 2
-    tops, denoms = [], []
-    for k in range(n):
-        both = r3[k, 8:16, :]
-        tops.append(jnp.where(near, both, pltpu.roll(both, HD // 2, 1)))
-        denoms.append(jnp.where(near, pltpu.roll(both, W - HD // 2, 1), both))
-    top = functools.reduce(jnp.maximum, tops, own)
+    all_back.wait()
+    pieces = back[...].astype(F32).reshape(n * n, 2, 8, W)
+    numers = pieces[:, 0].reshape(n * n * 8, W)
+    stats = pieces[:, 1].reshape(n * n * 8, W)
+    stats = stats + pltpu.roll(stats, W - 16, 1)
+    top = jnp.maximum(jnp.max(stats.reshape(n * n, 8, W), axis=0), own)
+    lead = lax.rem(lane8, HD) < 16
+    top = jnp.where(lead, top, 0.0)
+    factor = jnp.where(lead[None], jnp.exp(stats.reshape(n * n, 8, W) - top[None]), 0.0).reshape(n * n * 8, W)
+    factor = factor + pltpu.roll(factor, 16, 1)
+    factor = factor + pltpu.roll(factor, 32, 1)
+    numer = jnp.sum((numers * factor).reshape(n * n, 8, W), axis=0)
+    denom = jnp.sum((stats * factor).reshape(n * n, 8, W), axis=0)
+    top = top + pltpu.roll(top, 16, 1)
+    top = top + pltpu.roll(top, 32, 1)
+    denom = jnp.where((lax.rem(lane8, HD) >= 32) & (lax.rem(lane8, HD) < 48), denom, 0.0)
+    denom = denom + pltpu.roll(denom, 16, 1)
+    denom = denom + pltpu.roll(denom, W - 32, 1)
     own_weight = jnp.exp(own - top)
-    denom = own_weight
-    numer = own_weight.astype(BF16).astype(F32) * v8
-    for k in range(n):
-        factor = jnp.exp(tops[k] - top)
-        denom = denom + denoms[k] * factor
-        numer = numer + r3[k, 0:8, :] * factor
+    denom = denom + own_weight
+    numer = numer + own_weight.astype(BF16).astype(F32) * v8
     attended = (numer / denom).astype(BF16).astype(F32)
     attended = jnp.concatenate([jnp.where(upper, attended, 0.0), jnp.where(upper, 0.0, attended)], axis=1)
     part = dot(attended.astype(BF16), wo[...])
@@ -375,10 +376,11 @@
         got5[k - 1].wait_recv()
         summed = summed + xr[k]
     summed = (summed + res[hd]).astype(BF16)
-    out[:, 0:W] = summed[0:RD]
-    out[:, W : 2 * W] = summed[RD : 2 * RD]
+    outs[0, :, 0:W] = summed[0:RD]
+    outs[0, :, W : 2 * W] = summed[RD : 2 * RD]
     for copy in sends:
         copy.wait_send()
+    pltpu.make_async_copy(back_s.at[others], back.at[others], bs_sem).wait()
 
 
 def shards(
@@ -407,13 +409,13 @@
     vmem = pl.BlockSpec(memory_space=pltpu.VMEM)
     hbm = pl.BlockSpec(memory_space=pltpu.HBM)
     shape = jax.ShapeDtypeStruct
-    new = shape((RD, cols), BF16)
+    new = shape((3, RD, cols), BF16)
     dma = pltpu.SemaphoreType.DMA
-    return pl.pallas_call(
+    packed = pl.pallas_call(
         functools.partial(kernel, side, heads_n),
-        out_shape=(new, new, new),
+        out_shape=new,
         in_specs=[hbm] * 13,
-        out_specs=(vmem, vmem, vmem),
+        out_specs=vmem,
         scratch_shapes=[
             pltpu.VMEM((RD, d_model), BF16),
             pltpu.VMEM((1, d_model), F32),
@@ -428,18 +430,16 @@
             pltpu.VMEM((cols, d_model), BF16),
             pltpu.VMEM((2 * SL, BT, cols), BF16),
             pltpu.VMEM((2 * SL, BT, cols), BF16),
-            pltpu.VMEM((cols, 2 * SL * BT), BF16),
             pltpu.VMEM((2 * RD, d_model), F32),
             pltpu.VMEM((n, 2 * RD, W), F32),
             pltpu.VMEM((n, rows, W), BF16),
             pltpu.VMEM((8, W), F32),
             pltpu.VMEM((8, W), F32),
             pltpu.VMEM((1, nodes), F32),
-            pltpu.VMEM((8, n * lanes), F32),
-            pltpu.VMEM((n, HD + 16, lanes), BF16),
-            pltpu.VMEM((n, HD + 16, lanes), BF16),
-            pltpu.VMEM((n, 16, W), F32),
-            pltpu.VMEM((n, 16, W), F32),
+            pltpu.VMEM((n * rows, request_leaf.shape[0]), BF16),
+            pltpu.VMEM((n, rows, 2 * SL * BT), F32),
+            pltpu.VMEM((n * n, 16, W), BF16),
+            pltpu.VMEM((n * n, 16, W), BF16),
             pltpu.VMEM((heads_n, 8, W), F32),
             pltpu.VMEM((heads_n, 8, W), F32),
             pltpu.VMEM((heads_n, 8, W), F32),
@@ -447,7 +447,8 @@
             dma((3,)),
             dma((3,)),
         ]
-        + [dma((n,))] * 8
+        + [dma((n,))] * 4
+        + [dma(()), dma(())]
         + [dma((heads_n,))] * 2,
         compiler_params=pltpu.CompilerParams(
             collective_id=0, has_side_effects=True, vmem_limit_bytes=60 * 1024 * 1024
@@ -467,6 +468,7 @@
         cache_keys,
         cache_values,
     )
+    return packed[0], packed[1], packed[2]
 
 
 def solution(mesh):

time: 45.2 us -> 40.5 us (0.90)
  the two profiles are of different devices: /device:TPU:24 before, /device:TPU:8 now
where the time goes in v2:
time: 40.5 us; the launch traced here: 40.2 us
  Pallas kernels  37.7 us (93%)
  between operations  1.29 us (3%)
  local copies, waits for them, and re-layouts  1.27 us (3%)
    pallas_call x1, Pallas kernels, shards(): pl.pallas_call(functools.partial(kernel, side, heads_n), out_shape=new, i...  37.7 us
    squeeze x1, local copies, waits for them, and re-layouts, shards(): return (packed[0], packed[1], packed[2])  1.27 us

profile of v2, /device:TPU:8, one launch (start us, length us, event | category | flops | bytes accessed | tf_op | source)
XLA Modules:
  0.0 40.2 jit_solution(11299777862137250513)
XLA Ops:
  1.3 37.7 %shard_map.148 = bf16[3,4,256]{2,1,0:T(4,128)(2,1)} custom-call(bf16[4,1024]{1,0:T(4,128)(2,1)} %hidden_h.1, f32[1,1024]{1,0:T(1,128)} %bitcast.13, s32[1,168]{1,0:T(1,128)} %bitcast.15, s32[1,512]{1,0:T(1,128)} %bitcast.14, s32[1,2]{1,0:T(1,128)} %bitcast.16, s32[1,2]{1,0:T(1,128)} %bitcast.17, s32[1,1]{1,0:T(1,128)} %bitcast.12.live_h, ...), custom_call_target="tpu_custom_call" | custom-call | tf_op jit(solution)/shard_map/pallas_call | solution.py:414
  39.0 1.3 %slice_bitcast_fusion = (bf16[4,256]{1,0:T(4,128)(2,1)}, bf16[4,256]{1,0:T(4,128)(2,1)}, bf16[4,256]{1,0:T(4,128)(2,1)}) fusion(bf16[3,4,256]{2,1,0:T(4,128)(2,1)} %shard_map.148), kind=kLoop, calls=%fused_computation | loop fusion | bytes 12288 | tf_op jit(solution)/shard_map/squeeze | solution.py:471

commit v3 on v2

--- a/solution.py
+++ b/solution.py
@@ -37,13 +37,13 @@
 def kernel(
     side,
     heads_n,
+    live,
     hidden_h,
     gain_h,
     parent_h,
     leaf_h,
     node_h,
     len_h,
-    live_h,
     wq_h,
     wk_h,
     wv_h,
@@ -57,7 +57,6 @@
     leaf,
     node,
     length,
-    live,
     wq,
     wk,
     wv,
@@ -122,15 +121,8 @@
 
     other = {"blk": me + 1 - 2 * core, "head": hd}
 
-    barrier = pltpu.get_barrier_semaphore()
-    for k in range(1, n):
-        pl.semaphore_signal(barrier, inc=1, device_id=along_b(k), device_id_type=MESH)
-    for k in range(1, n):
-        pl.semaphore_signal(barrier, inc=1, device_id=along_a(k), device_id_type=MESH)
-    pl.semaphore_signal(barrier, inc=1, device_id=other, device_id_type=MESH)
-    for k in range(1, heads_n):
-        pl.semaphore_signal(barrier, inc=1, device_id=along_x(k), device_id_type=MESH)
-
+    order = sorted(range(1, n), key=lambda k: -min(k, n - k))
+    xorder = sorted(range(1, heads_n), key=lambda k: -min(k, heads_n - k))
     loads = [
         pltpu.make_async_copy(src, dst, lsem.at[k])
         for k, (src, dst) in enumerate(
@@ -140,7 +132,6 @@
                 (wq_h, wq),
                 (node_h, node),
                 (len_h, length),
-                (live_h, live),
                 (wk_h, wk),
                 (wv_h, wv),
                 (cv_h, vbuf.at[pl.ds(0, SL)]),
@@ -151,7 +142,18 @@
             ]
         )
     ]
-    for load in loads:
+    for load in loads[:3]:
+        load.start()
+
+    barrier = pltpu.get_barrier_semaphore()
+    for k in order:
+        pl.semaphore_signal(barrier, inc=1, device_id=along_b(k), device_id_type=MESH)
+    for k in order:
+        pl.semaphore_signal(barrier, inc=1, device_id=along_a(k), device_id_type=MESH)
+    pl.semaphore_signal(barrier, inc=1, device_id=other, device_id_type=MESH)
+    for k in xorder:
+        pl.semaphore_signal(barrier, inc=1, device_id=along_x(k), device_id_type=MESH)
+    for load in loads[3:]:
         load.start()
 
     loads[0].wait()
@@ -173,9 +175,9 @@
     q8 = tile_of(dot(normed, wq[...]).astype(BF16).astype(F32))
     g1[0] = q8
 
-    for k in (3, 4, 5):
+    for k in (3, 4):
         loads[k].wait()
-    own_len = [jnp.where(s < live[:, 0:1], length[:, s : s + 1], 0).astype(F32) for s in range(SL)]
+    own_len = [jnp.where(s < live[0], length[:, s : s + 1], 0).astype(F32) for s in range(SL)]
     own_node = [node[:, s : s + 1].astype(F32) for s in range(SL)]
 
     def slot_tile(first):
@@ -205,16 +207,15 @@
 
     pl.semaphore_wait(barrier, 2 * (n - 1) + 1 + heads_n - 1)
 
-    order = sorted(range(1, n), key=lambda k: -min(k, n - k))
     got1 = {k: send(g1.at[0], g1.at[k], g1s_sem.at[k], g1r_sem.at[k], along_b(k)) for k in order}
     got_meta = send(meta_send, meta_recv, csem.at[0], crem.at[0], other)
     got_v = send(cv_h, vbuf.at[pl.ds(SL, SL)], csem.at[1], crem.at[1], other)
     got_k = send(ck_h, kbuf.at[pl.ds(SL, SL)], csem.at[2], crem.at[2], other)
 
-    loads[6].wait()
+    loads[5].wait()
     k8 = dot(normed, wk[...]).astype(BF16)
     outs[1] = k8[0:RD, :]
-    loads[7].wait()
+    loads[6].wait()
     v8 = dot(normed, wv[...]).astype(BF16)
     outs[2] = v8[0:RD, :]
     k8 = tile_of(k8.astype(F32))
@@ -242,8 +243,8 @@
     g2[0] = g1[...].reshape(rows, W).astype(BF16)
     got2 = {k: send(g2.at[0], g2.at[k], g2s_sem.at[k], g2r_sem.at[k], along_a(k)) for k in order}
 
+    loads[9].wait()
     loads[10].wait()
-    loads[11].wait()
     par[...] = jnp.full_like(par, -1.0)
     par[:, 0 : parent.shape[1]] = parent[...].astype(F32)
     node_of_row = iota((nodes, 1), 0).astype(F32)
@@ -273,10 +274,10 @@
     ).astype(BF16)
     bias[...] = dot(unseen, hide).reshape(n, rows, tokens)
 
-    loads[8].wait()
+    loads[7].wait()
     got_v.wait_recv()
     values = vbuf[...].reshape(tokens, 2 * W)
-    loads[9].wait()
+    loads[8].wait()
     got_k.wait_recv()
     keys = kbuf[...].reshape(tokens, 2 * W)
 
@@ -340,7 +341,7 @@
             send(back_s.at[slot], back.at[slot], bs_sem, br_sem, plane(-k, -j), False)
     others = pl.ds(1, n * n - 1)
     all_back = pltpu.make_async_copy(back_s.at[others], back.at[others], br_sem)
-    loads[12].wait()
+    loads[11].wait()
     all_back.wait()
     pieces = back[...].astype(F32).reshape(n * n, 2, 8, W)
     numers = pieces[:, 0].reshape(n * n * 8, W)
@@ -368,12 +369,12 @@
     part = part + pltpu.roll(part, RD, 0)
     for k in range(heads_n):
         xs[k] = tile_of(part[:, 2 * W * k : 2 * W * (k + 1)])
-    got5 = [
-        send(xs.at[(hd + k) % heads_n], xr.at[k], xs_sem.at[k], xr_sem.at[k], along_x(k)) for k in range(1, heads_n)
-    ]
+    got5 = {
+        k: send(xs.at[(hd + k) % heads_n], xr.at[k], xs_sem.at[k], xr_sem.at[k], along_x(k)) for k in xorder
+    }
     summed = xs[hd]
     for k in range(1, heads_n):
-        got5[k - 1].wait_recv()
+        got5[k].wait_recv()
         summed = summed + xr[k]
     summed = (summed + res[hd]).astype(BF16)
     outs[0, :, 0:W] = summed[0:RD]
@@ -414,7 +415,7 @@
     packed = pl.pallas_call(
         functools.partial(kernel, side, heads_n),
         out_shape=new,
-        in_specs=[hbm] * 13,
+        in_specs=[pl.BlockSpec(memory_space=pltpu.SMEM)] + [hbm] * 12,
         out_specs=vmem,
         scratch_shapes=[
             pltpu.VMEM((RD, d_model), BF16),
@@ -423,7 +424,6 @@
             pltpu.VMEM((1, request_leaf.shape[0]), jnp.int32),
             pltpu.VMEM((1, SL), jnp.int32),
             pltpu.VMEM((1, SL), jnp.int32),
-            pltpu.VMEM((1, 1), jnp.int32),
             pltpu.VMEM((d_model, cols), BF16),
             pltpu.VMEM((d_model, cols), BF16),
             pltpu.VMEM((d_model, cols), BF16),
@@ -443,7 +443,7 @@
             pltpu.VMEM((heads_n, 8, W), F32),
             pltpu.VMEM((heads_n, 8, W), F32),
             pltpu.VMEM((heads_n, 8, W), F32),
-            dma((13,)),
+            dma((12,)),
             dma((3,)),
             dma((3,)),
         ]
@@ -451,23 +451,29 @@
         + [dma(()), dma(())]
         + [dma((heads_n,))] * 2,
         compiler_params=pltpu.CompilerParams(
-            collective_id=0, has_side_effects=True, vmem_limit_bytes=60 * 1024 * 1024
+            collective_id=0, has_side_effects=True, vmem_limit_bytes=48 * 1024 * 1024
         ),
     )(
-        hidden_in,
-        norm_gain.reshape(1, -1),
-        node_parent.reshape(1, -1),
-        request_leaf.reshape(1, -1),
-        block_node.reshape(1, -1),
-        block_len.reshape(1, -1),
-        live_count.reshape(1, -1),
-        w_query,
-        w_key,
-        w_value,
-        w_out,
-        cache_keys,
-        cache_values,
+        live_count,
+        *(
+            pltpu.with_memory_space_constraint(x, pltpu.HBM)
+            for x in (
+                hidden_in,
+                norm_gain.reshape(1, -1),
+                node_parent.reshape(1, -1),
+                request_leaf.reshape(1, -1),
+                block_node.reshape(1, -1),
+                block_len.reshape(1, -1),
+                w_query,
+                w_key,
+                w_value,
+                w_out,
+                cache_keys,
+                cache_values,
+            )
+        )
     )
+
     return packed[0], packed[1], packed[2]
 
 

time: 40.5 us -> 39.1 us (0.965)
  Pallas kernels: 37.7 us -> 37 us
  local copies, waits for them, and re-layouts: 1.27 us -> 0.59 us
    squeeze x1, local copies, waits for them, and re-layouts: 1.27 us -> 0.59 us  [shards(): return (packed[0], packed[1], packed[2])]
    pallas_call x1, Pallas kernels: 37.7 us -> 37 us  [shards(): pl.pallas_call(functools.partial(kernel, side, heads_n), out_shape=new, i...]
where the time goes in v3:
time: 39.1 us; the launch traced here: 38.9 us
  Pallas kernels  37 us (95%)
  between operations  1.29 us (3%)
  local copies, waits for them, and re-layouts  0.59 us (2%)
    pallas_call x1, Pallas kernels, shards(): pl.pallas_call(functools.partial(kernel, side, heads_n), out_shape=new, i...  37 us

profile of v3, /device:TPU:8, one launch (start us, length us, event | category | flops | bytes accessed | tf_op | source)
XLA Modules:
  0.0 38.9 jit_solution(3817273756059262751)
XLA Ops:
  1.3 37.0 %shard_map.148 = bf16[3,4,256]{2,1,0:T(4,128)(2,1)S(1)} custom-call(s32[1]{0:T(128)S(6)} %copy.16.live, bf16[4,1024]{1,0:T(4,128)(2,1)} %hidden_h.1, f32[1,1024]{1,0:T(1,128)} %bitcast.11, s32[1,168]{1,0:T(1,128)} %bitcast.13, s32[1,512]{1,0:T(1,128)} %bitcast.12, s32[1,2]{1,0:T(1,128)} %bitcast.14, s32[1,2]{1,0:T(1,128)} %bitcast.15, ...), custom_call_target="tpu_custom_call" | custom-call | tf_op jit(solution)/shard_map/pallas_call | solution.py:415
  38.3 0.6 %slice_bitcast_fusion = (bf16[4,256]{1,0:T(4,128)(2,1)}, bf16[4,256]{1,0:T(4,128)(2,1)}, bf16[4,256]{1,0:T(4,128)(2,1)}) fusion(bf16[3,4,256]{2,1,0:T(4,128)(2,1)S(1)} %shard_map.148), kind=kLoop, calls=%fused_computation | loop fusion | bytes 12288 | tf_op jit(solution)/shard_map/squeeze | solution.py:477

commit v4 on v3

--- a/solution.py
+++ b/solution.py
@@ -329,6 +329,12 @@
 
     returned = None
     reach = [min(k, n - k) for k in range(n)]
+    low = max(1, n * 3 // 8)
+    high = max(low + 1, n * 6 // 8)
+
+    def part_at(k):
+        return 0 if k < low else 1 if k < high else 2
+
     batches = BATCHES8 if n == 8 else (tuple(range(n)),)
     for batch in batches:
         for k in batch:
@@ -338,25 +344,44 @@
         pairs = [(k, j) for k in batch for j in range(n) if k or j]
         for k, j in sorted(pairs, key=lambda p: -reach[p[0]] - reach[p[1]]):
             slot = n * k + j
-            send(back_s.at[slot], back.at[slot], bs_sem, br_sem, plane(-k, -j), False)
-    others = pl.ds(1, n * n - 1)
-    all_back = pltpu.make_async_copy(back_s.at[others], back.at[others], br_sem)
+            send(back_s.at[slot], back.at[slot], bs_sem, br_sem.at[part_at(k)], plane(-k, -j), False)
     loads[11].wait()
-    all_back.wait()
-    pieces = back[...].astype(F32).reshape(n * n, 2, 8, W)
-    numers = pieces[:, 0].reshape(n * n * 8, W)
-    stats = pieces[:, 1].reshape(n * n * 8, W)
-    stats = stats + pltpu.roll(stats, W - 16, 1)
-    top = jnp.maximum(jnp.max(stats.reshape(n * n, 8, W), axis=0), own)
+    for copy in sends:
+        copy.wait_send()
+    sends.clear()
     lead = lax.rem(lane8, HD) < 16
-    top = jnp.where(lead, top, 0.0)
-    factor = jnp.where(lead[None], jnp.exp(stats.reshape(n * n, 8, W) - top[None]), 0.0).reshape(n * n * 8, W)
-    factor = factor + pltpu.roll(factor, 16, 1)
-    factor = factor + pltpu.roll(factor, 32, 1)
-    numer = jnp.sum((numers * factor).reshape(n * n, 8, W), axis=0)
-    denom = jnp.sum((stats * factor).reshape(n * n, 8, W), axis=0)
-    top = top + pltpu.roll(top, 16, 1)
-    top = top + pltpu.roll(top, 32, 1)
+
+    def spread(x):
+        x = x + pltpu.roll(x, 16, x.ndim - 1)
+        return x + pltpu.roll(x, 32, x.ndim - 1)
+
+    def merge(spans):
+        parts = []
+        for which, begin, end in spans:
+            if begin < end:
+                here = pl.ds(max(begin, 1), end - max(begin, 1))
+                pltpu.make_async_copy(back.at[here], back.at[here], br_sem.at[which]).wait()
+                parts.append(back[begin:end].astype(F32))
+        pieces = jnp.concatenate(parts, axis=0)
+        count = pieces.shape[0]
+        pieces = pieces.reshape(count, 2, 8, W)
+        stats = pieces[:, 1].reshape(count * 8, W)
+        stats = stats + pltpu.roll(stats, W - 16, 1)
+        top = jnp.where(lead, jnp.max(stats.reshape(count, 8, W), axis=0), 0.0)
+        factor = jnp.where(lead[None], jnp.exp(stats.reshape(count, 8, W) - top[None]), 0.0)
+        factor = spread(factor.reshape(count * 8, W))
+        numer = jnp.sum((pieces[:, 0].reshape(count * 8, W) * factor).reshape(count, 8, W), axis=0)
+        denom = jnp.sum((stats * factor).reshape(count, 8, W), axis=0)
+        return top, numer, denom
+
+    near_top, near_numer, near_denom = merge([(0, 0, low * n), (2, high * n, n * n)])
+    far_top, far_numer, far_denom = merge([(1, low * n, high * n)])
+    top = jnp.where(lead, jnp.maximum(jnp.maximum(near_top, far_top), own), 0.0)
+    near_factor = spread(jnp.where(lead, jnp.exp(near_top - top), 0.0))
+    far_factor = spread(jnp.where(lead, jnp.exp(far_top - top), 0.0))
+    numer = near_numer * near_factor + far_numer * far_factor
+    denom = near_denom * near_factor + far_denom * far_factor
+    top = spread(top)
     denom = jnp.where((lax.rem(lane8, HD) >= 32) & (lax.rem(lane8, HD) < 48), denom, 0.0)
     denom = denom + pltpu.roll(denom, 16, 1)
     denom = denom + pltpu.roll(denom, W - 32, 1)
@@ -372,6 +397,8 @@
     got5 = {
         k: send(xs.at[(hd + k) % heads_n], xr.at[k], xs_sem.at[k], xr_sem.at[k], along_x(k)) for k in xorder
     }
+    others = pl.ds(1, n * n - 1)
+    pltpu.make_async_copy(back_s.at[others], back.at[others], bs_sem).wait()
     summed = xs[hd]
     for k in range(1, heads_n):
         got5[k].wait_recv()
@@ -381,7 +408,6 @@
     outs[0, :, W : 2 * W] = summed[RD : 2 * RD]
     for copy in sends:
         copy.wait_send()
-    pltpu.make_async_copy(back_s.at[others], back.at[others], bs_sem).wait()
 
 
 def shards(
@@ -448,7 +474,7 @@
             dma((3,)),
         ]
         + [dma((n,))] * 4
-        + [dma(()), dma(())]
+        + [dma(()), dma((3,))]
         + [dma((heads_n,))] * 2,
         compiler_params=pltpu.CompilerParams(
             collective_id=0, has_side_effects=True, vmem_limit_bytes=48 * 1024 * 1024

time: 39.1 us -> 39 us (level)
  no operation moved by 1% of the time
where the time goes in v4:
time: 39 us; the launch traced here: 38.8 us
  Pallas kernels  36.9 us (95%)
  between operations  1.29 us (3%)
  local copies, waits for them, and re-layouts  0.59 us (2%)
    pallas_call x1, Pallas kernels, shards(): pl.pallas_call(functools.partial(kernel, side, heads_n), out_shape=new, i...  36.9 us

profile of v4, /device:TPU:8, one launch (start us, length us, event | category | flops | bytes accessed | tf_op | source)
XLA Modules:
  0.0 38.8 jit_solution(3523352619101679573)
XLA Ops:
  1.3 36.9 %shard_map.148 = bf16[3,4,256]{2,1,0:T(4,128)(2,1)S(1)} custom-call(s32[1]{0:T(128)S(6)} %copy.16.live, bf16[4,1024]{1,0:T(4,128)(2,1)} %hidden_h.1, f32[1,1024]{1,0:T(1,128)} %bitcast.11, s32[1,168]{1,0:T(1,128)} %bitcast.13, s32[1,512]{1,0:T(1,128)} %bitcast.12, s32[1,2]{1,0:T(1,128)} %bitcast.14, s32[1,2]{1,0:T(1,128)} %bitcast.15, ...), custom_call_target="tpu_custom_call" | custom-call | tf_op jit(solution)/shard_map/pallas_call | solution.py:441
  38.2 0.6 %slice_bitcast_fusion = (bf16[4,256]{1,0:T(4,128)(2,1)}, bf16[4,256]{1,0:T(4,128)(2,1)}, bf16[4,256]{1,0:T(4,128)(2,1)}) fusion(bf16[3,4,256]{2,1,0:T(4,128)(2,1)S(1)} %shard_map.148), kind=kLoop, calls=%fused_computation | loop fusion | bytes 12288 | tf_op jit(solution)/shard_map/squeeze | solution.py:503

commit v5 on v4

--- a/solution.py
+++ b/solution.py
@@ -19,7 +19,7 @@
 
 very_low = -1e30
 low_top = -1e29
-BATCHES8 = ((0, 1, 7), (2, 6), (3, 5, 4))
+BATCHES8 = ((0,), (1, 7), (2, 6), (3, 5, 4))
 
 
 def iota(shape, axis):

time: 39 us -> 39.1 us (level)
  no operation moved by 1% of the time
where the time goes in v5:
time: 39.1 us; the launch traced here: 38.9 us
  Pallas kernels  37 us (95%)
  between operations  1.29 us (3%)
  local copies, waits for them, and re-layouts  0.59 us (2%)
    pallas_call x1, Pallas kernels, shards(): pl.pallas_call(functools.partial(kernel, side, heads_n), out_shape=new, i...  37 us

profile of v5, /device:TPU:8, one launch (start us, length us, event | category | flops | bytes accessed | tf_op | source)
XLA Modules:
  0.0 38.9 jit_solution(1817383441780841829)
XLA Ops:
  1.3 37.0 %shard_map.148 = bf16[3,4,256]{2,1,0:T(4,128)(2,1)S(1)} custom-call(s32[1]{0:T(128)S(6)} %copy.16.live, bf16[4,1024]{1,0:T(4,128)(2,1)} %hidden_h.1, f32[1,1024]{1,0:T(1,128)} %bitcast.11, s32[1,168]{1,0:T(1,128)} %bitcast.13, s32[1,512]{1,0:T(1,128)} %bitcast.12, s32[1,2]{1,0:T(1,128)} %bitcast.14, s32[1,2]{1,0:T(1,128)} %bitcast.15, ...), custom_call_target="tpu_custom_call" | custom-call | tf_op jit(solution)/shard_map/pallas_call | solution.py:441
  38.3 0.6 %slice_bitcast_fusion = (bf16[4,256]{1,0:T(4,128)(2,1)}, bf16[4,256]{1,0:T(4,128)(2,1)}, bf16[4,256]{1,0:T(4,128)(2,1)}) fusion(bf16[3,4,256]{2,1,0:T(4,128)(2,1)S(1)} %shard_map.148), kind=kLoop, calls=%fused_computation | loop fusion | bytes 12288 | tf_op jit(solution)/shard_map/squeeze | solution.py:503
